TPU v7x, 256 devices: a whole 4x4x8 slice. The times are simulated.
256 devices in a mesh: seq: 64 (over x, z, core), tp: 4 (over y).
Axes of the slice: x: 4, y: 4, z: 8, core: 2. Of those that a mesh axis runs over, the one named last changes fastest.
Arguments:
- token_ids: int32 [65536], P('seq'), may hold values from 0 to 511
- embed_table: bfloat16 [512, 2048], P(None, 'tp'), may hold values from -6 to 6
- norm_gain: float32 [2048], replicated, may hold values from 0.1 to 1.9
- in_weight: bfloat16 [2048, 3, 2048], P('seq', None, 'tp'), may hold values from -0.125 to 0.125
- short_filter: float32 [7, 3, 2048], P(None, None, 'tp'), may hold values from -2.4 to 2.4
- long_filter: bfloat16 [128, 128], P('tp'), may hold values from -0.5390625 to 0.5390625
- long_skip: float32 [2048], P('tp'), may hold values from -3 to 3
- out_weight: bfloat16 [2048, 2048], P('tp', 'seq'), may hold values from -0.125 to 0.125
Outputs:
- mixed: bfloat16 [65536, 2048], P('seq', 'tp')
All inputs are finite; a program needn't handle non-finite values.
Results may differ from a plain program's by a relative error of at most 0.012.
Values may be sent and summed in bfloat16 or wider, within the bound.
A program may use at most 64 MiB of HBM per device.

v0:
```python
import jax
import jax.numpy as jnp
from jax import lax
from jax.sharding import PartitionSpec as P


def from_behind(block, axis, distance):
    devices = range(lax.axis_size(axis))
    route = [(i - distance, i) for i in devices if i - distance in devices]
    return lax.ppermute(block, axis, route)


def short_conv(extended, short_filter, out_length):
    short_taps = short_filter.shape[0]
    running = jnp.zeros((out_length,) + extended.shape[1:], jnp.float32)
    for tap_index in range(short_taps):
        begin = short_taps - 1 - tap_index
        running = running + short_filter[tap_index][None] * extended[
            begin : begin + out_length
        ].astype(jnp.float32)
    return running


def body(
    token_ids, embed_table, norm_gain, in_weight, short_filter, long_filter, long_skip, out_weight
):
    tok_count = token_ids.shape[0]
    vocab_size = embed_table.shape[0]
    local_width = embed_table.shape[1]
    onehot = (token_ids[:, None] == jnp.arange(vocab_size, dtype=jnp.int32)[None, :]).astype(
        jnp.bfloat16
    )
    own_feats = jnp.dot(onehot, embed_table, preferred_element_type=jnp.float32).astype(
        jnp.bfloat16
    )
    features = lax.all_gather(own_feats, "tp", axis=1, tiled=True)
    widened = features.astype(jnp.float32)
    scaled = (
        widened
        * lax.rsqrt(jnp.mean(widened * widened, axis=1, keepdims=True) + 1e-06)
        * norm_gain[None, :]
    )
    normed = scaled.astype(jnp.bfloat16)
    projected = jnp.einsum(
        "td,dsc->tsc",
        normed,
        lax.all_gather(in_weight, "seq", axis=0, tiled=True),
        preferred_element_type=jnp.float32,
    ).astype(jnp.bfloat16)
    tap_count = long_filter.shape[1]
    short_taps = short_filter.shape[0]
    rim_rows = from_behind(projected[tok_count - short_taps + 1 :], "seq", 1)
    extended = jnp.concatenate([rim_rows, projected], axis=0)
    featured = short_conv(extended, short_filter, tok_count)
    queries = featured[:, 0]
    gated_kv = (featured[:, 1] * featured[:, 2]).astype(jnp.bfloat16)
    earlier = from_behind(gated_kv[tok_count - tap_count :], "seq", 1)
    product = jnp.concatenate([earlier, gated_kv], axis=0)
    groups_here = long_filter.shape[0]
    group_size = local_width // groups_here
    positions = jnp.arange(tap_count, dtype=jnp.int32)
    differ = positions[:, None, None] - positions[None, :, None]
    target = positions[None, None, :]
    near_pick = (differ == target).astype(jnp.float32)
    far_pick = (differ + tap_count == target).astype(jnp.float32)
    filter_f32 = long_filter.astype(jnp.float32)
    near_band = jnp.einsum("isj,gj->gis", near_pick, filter_f32).astype(jnp.bfloat16)
    far_band = jnp.einsum("isj,gj->gis", far_pick, filter_f32).astype(jnp.bfloat16)
    blocks = product.reshape(tok_count // tap_count + 1, tap_count, groups_here, group_size)
    convolved = jnp.einsum(
        "gis,bsgc->bigc", near_band, blocks[1:], preferred_element_type=jnp.float32
    )
    convolved = convolved + jnp.einsum(
        "gis,bsgc->bigc", far_band, blocks[:-1], preferred_element_type=jnp.float32
    )
    convolved = convolved.reshape(tok_count, local_width) + long_skip[None, :] * product[
        tap_count:
    ].astype(jnp.float32)
    gated = (queries * convolved).astype(jnp.bfloat16)
    partials = jnp.dot(
        gated,
        lax.all_gather(out_weight, "seq", axis=1, tiled=True),
        preferred_element_type=jnp.float32,
    )
    summed = lax.psum(partials.astype(jnp.bfloat16), "tp").astype(jnp.float32)
    own_share = lax.dynamic_slice_in_dim(summed, lax.axis_index("tp") * local_width, local_width, 1)
    return (own_feats.astype(jnp.float32) + own_share).astype(jnp.bfloat16)


def solution(mesh):
    placed = (
        P("seq"),
        P(None, "tp"),
        P(),
        P("seq", None, "tp"),
        P(None, None, "tp"),
        P("tp", None),
        P("tp"),
        P("tp", "seq"),
    )
    return jax.shard_map(
        body, mesh=mesh, in_specs=placed, out_specs=P("seq", "tp"), check_vma=False
    )
```

profile of v0, /device:TPU:1, one launch (start us, length us, event | category | flops | bytes accessed | tf_op | source)
XLA Modules:
  0.0 337.5 jit_solution(16231888260444834584)
XLA Ops:
  6.5 1.0 copy-done
  7.6 2.4 fusion.24
  10.1 0.7 all-gather.6.cloned.1.call-update
  10.8 0.7 all-gather.8.cloned.1.call-update
  11.6 1.2 fusion.38
  12.8 5.8 %fusion.3 = bf16[128,128,32]{1,2,0:T(8,128)(2,1)} fusion(s32[128,128]{1,0:T(8,128)S(1)} %iota_subtract_fusion, bf16[32,128]{1,0:T(8,128)(2,1)} %param.13), kind=kOutput, calls=%fused_computation.7 | convolution fusion | flops 136314880 | bytes 1122304 | tf_op jit(solution)/shard_map/isj,gj->gis/dot_general | solution.py:67
  18.6 5.1 %fusion.4 = bf16[128,128,32]{1,2,0:T(8,128)(2,1)} fusion(s32[128,128]{1,0:T(8,128)S(1)} %broadcast_add_fusion, bf16[32,128]{1,0:T(8,128)(2,1)S(1)} %copy-done.5), kind=kOutput, calls=%fused_computation.8 | convolution fusion | flops 136314880 | bytes 1122304 | tf_op jit(solution)/shard_map/isj,gj->gis/dot_general | solution.py:68
  23.7 40.8 %all-gather.4.cloned.1.call-done = bf16[1024,2048]{1,0:T(8,128)(2,1)} async-done(((bf16[1024,512]{1,0:T(8,128)(2,1)}), bf16[1024,2048]{1,0:T(8,128)(2,1)}) %all-gather.4.cloned.1.call-update) | async-done | bytes 4194320 | tf_op jit(solution)/shard_map/all_gather | solution.py:36
  64.6 3.1 fusion
  67.7 81.2 %all-gather.6.cloned.1.call-done = bf16[2048,3,512]{2,0,1:T(8,128)(2,1)} async-done(((bf16[32,3,512]{2,0,1:T(8,128)(2,1)}), bf16[2048,3,512]{2,0,1:T(8,128)(2,1)}) %all-gather.6.cloned.1.call-update) | async-done | bytes 6291472 | tf_op jit(solution)/shard_map/all_gather | solution.py:47
  148.8 10.5 %fusion.17 = bf16[1024,3,512]{2,0,1:T(8,128)(2,1)S(1)} fusion(bf16[2048,3,512]{2,0,1:T(8,128)(2,1)} %all-gather.6.cloned.1.call-done, bf16[1024,2048]{1,0:T(8,128)(2,1)} %all-gather.4.cloned.1.call-done, f32[2048]{0:T(1024)S(1)} %copy-done.6, f32[1024]{0:T(1024)S(1)} %add_rsqrt_fusion), kind=kOutput, calls=%fused_computation.31 | convolution fusion | flops 6452412416 | bytes 13643776 | tf_op jit(solution)/shard_map/td,dsc->tsc/dot_general | solution.py:44
  159.4 2.8 collective-permute-start
  162.2 0.9 collective-permute-done
  163.1 5.6 %multiply_add_fusion = f32[1024,3,512]{2,0,1:T(8,128)S(1)} fusion(bf16[1024,3,512]{2,0,1:T(8,128)(2,1)S(1)} %fusion.17, bf16[6,3,512]{2,0,1:T(8,128)(2,1)S(1)} %collective-permute-done, f32[3,512]{1,0:T(4,128)S(1)} %get-tuple-element.12, f32[3,512]{1,0:T(4,128)S(1)} %get-tuple-element.13, f32[3,512]{1,0:T(4,128)S(1)} %get-tuple-element.14, ...), kind=kLoop, calls=%fused_computation.14 | loop fusion | flops 59768832 | bytes 9498624 | tf_op jit(solution)/shard_map/add | solution.py:18
  168.7 2.7 copy-done.1
  171.3 0.4 fusion.20
  171.7 0.5 copy.12
  172.3 4.7 %collective-permute-start.1 = (bf16[128,512]{1,0:T(8,128)(2,1)S(1)}, bf16[128,512]{1,0:T(8,128)(2,1)S(1)}, u32[]{:S(2)}, u32[]{:S(2)}) collective-permute-start(bf16[128,512]{1,0:T(8,128)(2,1)S(1)} %slice_bitcast_fusion.1), channel_id=1, source_target_pairs={{0,4},{4,8},{8,12},{12,16},{16,20},{20,24},{24,28},{28,32},{32,36}... | collective-permute-start | bytes 393224 | tf_op jit(solution)/shard_map/ppermute | solution.py:10
  176.9 0.3 copy.29
  177.2 2.1 fusion.26
  179.3 0.4 fusion.42
  179.7 1.1 pad_maximum_fusion.1
  180.7 2.3 copy.14
  183.0 1.5 copy.30
  184.5 2.1 add_bitcast_fusion
  186.6 0.9 copy.16
  187.5 0.5 copy.52
  188.0 1.8 copy.17
  189.8 35.9 %all-gather.8.cloned.1.call-done = bf16[512,2048]{0,1:T(8,128)(2,1)} async-done(((bf16[512,32]{0,1:T(8,128)(2,1)}), bf16[512,2048]{0,1:T(8,128)(2,1)}) %all-gather.8.cloned.1.call-update) | async-done | bytes 2097168 | tf_op jit(solution)/shard_map/all_gather | solution.py:82
  225.7 7.6 %convolution_convert_fusion = bf16[1024,2048]{1,0:T(8,128)(2,1)} fusion(bf16[512,2048]{0,1:T(8,128)(2,1)} %all-gather.8.cloned.1.call-done, f32[1024,3,512]{2,0,1:T(8,128)} %copy-done.1, f32[1024,512]{1,0:T(8,128)} %copy.17, f32[512]{0:T(512)S(1)} %copy-done.7, bf16[1024,1,512]{2,0,1:T(8,128)(2,1)} %copy-done.3), kind=kOutput, calls=%fused_computation.21 | convolution fusion | flops 2152202240 | bytes 11536384 | tf_op jit(solution)/shard_map/dot_general | solution.py:80
  233.3 95.2 %all-reduce.2.cloned.1.call-done = bf16[1024,2048]{1,0:T(8,128)(2,1)} async-done(((bf16[1024,2048]{1,0:T(8,128)(2,1)}), bf16[1024,2048]{1,0:T(8,128)(2,1)}) %all-reduce.2.cloned.1.call-update) | async-done | bytes 4194320 | tf_op jit(solution)/shard_map/psum | solution.py:85
  328.5 2.5 add_convert_fusion
  (30 shorter events, 0.3 us)
Async XLA Ops:
  6.5 1.0 copy-start
  6.5 12.1 %copy-start.5 = (bf16[32,128]{1,0:T(8,128)(2,1)S(1)}, bf16[32,128]{1,0:T(8,128)(2,1)}, u32[]{:S(2)}) copy-start(bf16[32,128]{1,0:T(8,128)(2,1)} %param.13) | copy-start | bytes 24580
  6.5 58.0 %all-gather.4.cloned.1.call-start = ((), (), s32[]{:S(2)}) async-start(), calls=%async_computation | async-start | bytes 5242880 | tf_op jit(solution)/shard_map/all_gather | solution.py:36
  10.0 138.8 %all-gather.6.cloned.1.call-start = ((), (), s32[]{:S(2)}) async-start(), calls=%async_computation.1 | async-start | bytes 6389760 | tf_op jit(solution)/shard_map/all_gather | solution.py:47
  10.8 214.9 %all-gather.8.cloned.1.call-start = ((), (), s32[]{:S(2)}) async-start(), calls=%async_computation.2 | async-start | bytes 2129920 | tf_op jit(solution)/shard_map/all_gather | solution.py:82
  11.5 317.0 %all-reduce.2.cloned.1.call-start = ((), (), s32[]{:S(2)}) async-start(), calls=%async_computation.3 | async-start | bytes 8388608 | tf_op jit(solution)/shard_map/psum | solution.py:85
  12.8 136.0 %copy-start.6 = (f32[2048]{0:T(1024)S(1)}, f32[2048]{0:T(1024)}, u32[]{:S(2)}) copy-start(f32[2048]{0:T(1024)} %param.10) | copy-start | bytes 24580
  159.4 3.7 %collective-permute-start = (bf16[6,3,512]{2,0,1:T(8,128)(2,1)S(1)}, bf16[6,3,512]{2,0,1:T(8,128)(2,1)S(1)}, u32[]{:S(2)}, u32[]{:S(2)}) collective-permute-start(bf16[6,3,512]{2,0,1:T(8,128)(2,1)S(1)} %slice.86), channel_id=1, source_target_pairs={{0,4},{4,8},{8,12},{12,16},{16,20},{20,24},{24,28},{28,32},{32,36}... | collective-permute-start | bytes 55304 | tf_op jit(solution)/shard_map/ppermute | solution.py:10
  168.7 2.7 copy-start.1
  171.7 5.5 %copy-start.3 = (bf16[1024,1,512]{2,0,1:T(8,128)(2,1)}, bf16[1024,1,512]{2,0,1:T(8,128)(2,1)S(1)}, u32[]{:S(2)}) copy-start(bf16[1024,1,512]{2,0,1:T(8,128)(2,1)S(1)} %fusion.20) | copy-start | bytes 3145732
  172.2 7.1 %copy-start.2 = (f32[1024,3,512]{2,0,1:T(8,128)S(1)}, f32[1024,3,512]{2,0,1:T(8,128)}, u32[]{:S(2)}) copy-start(f32[1024,3,512]{2,0,1:T(8,128)} %copy-done.1) | copy-start | bytes 18874372
  172.3 7.4 %collective-permute-start.1 = (bf16[128,512]{1,0:T(8,128)(2,1)S(1)}, bf16[128,512]{1,0:T(8,128)(2,1)S(1)}, u32[]{:S(2)}, u32[]{:S(2)}) collective-permute-start(bf16[128,512]{1,0:T(8,128)(2,1)S(1)} %slice_bitcast_fusion.1), channel_id=1, source_target_pairs={{0,4},{4,8},{8,12},{12,16},{16,20},{20,24},{24,28},{28,32},{32,36}... | collective-permute-start | bytes 393224 | tf_op jit(solution)/shard_map/ppermute | solution.py:10
  186.6 39.1 %copy-start.7 = (f32[512]{0:T(512)S(1)}, f32[512]{0:T(512)}, u32[]{:S(2)}) copy-start(f32[512]{0:T(512)} %param.14) | copy-start | bytes 6148
  189.8 138.7 %copy-start.4 = (bf16[1024,512]{1,0:T(8,128)(2,1)S(1)}, bf16[1024,512]{1,0:T(8,128)(2,1)}, u32[]{:S(2)}) copy-start(bf16[1024,512]{1,0:T(8,128)(2,1)} %fusion.24) | copy-start | bytes 3145732
Sparse Core Ops, SparseCore 0:
  10.1 54.3 all-gather.3
  67.4 81.3 all-gather.5
  151.6 74.0 all-gather.7
  233.4 94.9 all-reduce.1
where the time goes:
time: 338 us; the launch traced here: 337 us
  waiting for transfers between devices  255 us (75%)
  matrix products  35.6 us (11%)
  between operations  13.3 us (4%)
  other arithmetic  12.9 us (4%)
  local copies, waits for them, and re-layouts  12.7 us (4%)
  starting transfers between devices  7.53 us (2%)
    psum x1, waiting for transfers between devices, body(): summed = lax.psum(partials.astype(jnp.bfloat16), 'tp').astype(jnp.float32)  95.2 us
    all_gather x1, waiting for transfers between devices, body(): lax.all_gather(in_weight, 'seq', axis=0, tiled=True)  81.2 us
    all_gather x1, waiting for transfers between devices, body(): features = lax.all_gather(own_feats, 'tp', axis=1, tiled=True)  40.8 us
    all_gather x1, waiting for transfers between devices, body(): lax.all_gather(out_weight, 'seq', axis=1, tiled=True)  35.9 us
    dot_general x1, matrix products, body(): jnp.einsum('td,dsc->tsc', normed, lax.all_gather(in_weight, 'seq', axis=0...  10.5 us
    dot_general x1, matrix products, body(): jnp.dot(gated, lax.all_gather(out_weight, 'seq', axis=1, tiled=True), pre...  7.59 us
    ppermute x2, starting transfers between devices, from_behind(): return lax.ppermute(block, axis, route)  7.41 us
  transfers between devices with their start and end apart: 6, of which 5 were waited for; matrix products, arithmetic and copies ran while one was open for 13% of the time, Pallas kernels for 0%

commit v1 on v0

--- a/solution.py
+++ b/solution.py
@@ -79,7 +79,9 @@
     gated = (queries * convolved).astype(jnp.bfloat16)
     partials = jnp.dot(
         gated,
-        lax.all_gather(out_weight, "seq", axis=1, tiled=True),
+        jnp.concatenate(
+            lax.all_to_all(jnp.stack([out_weight] * lax.axis_size("seq")), "seq", 0, 0), axis=1
+        ),
         preferred_element_type=jnp.float32,
     )
     summed = lax.psum(partials.astype(jnp.bfloat16), "tp").astype(jnp.float32)

time: 338 us -> 306 us (0.905)
  waiting for transfers between devices: 255 us -> 208 us
  starting transfers between devices: 7.53 us -> 20.6 us
  local copies, waits for them, and re-layouts: 12.7 us -> 16.1 us
    all_gather x1 -> x0, waiting for transfers between devices: 35.9 us -> none  [body(): lax.all_gather(out_weight, 'seq', axis=1, tiled=True)]
    all_to_all x0 -> x1, starting transfers between devices: none -> 13.2 us  [body(): lax.all_to_all(jnp.stack([out_weight] * lax.axis_size('seq')), 'seq', 0, 0)]
    all_gather x1, waiting for transfers between devices: 40.8 us -> 27.9 us  [body(): features = lax.all_gather(own_feats, 'tp', axis=1, tiled=True)]
  transfers between devices with their start and end apart: 6 -> 6, of which waited for: 5 -> 4; matrix products, arithmetic and copies ran while one was open for 13% -> 16% of each run, Pallas kernels for 0% -> 0%
where the time goes in v1:
time: 306 us
  waiting for transfers between devices  208 us (68%)
  matrix products  34.6 us (11%)
  starting transfers between devices  20.6 us (7%)
  local copies, waits for them, and re-layouts  16.1 us (5%)
  between operations  13.4 us (4%)
  other arithmetic  12.9 us (4%)
    psum x1, waiting for transfers between devices, body(): summed = lax.psum(partials.astype(jnp.bfloat16), 'tp').astype(jnp.float32)  97.2 us
    all_gather x1, waiting for transfers between devices, body(): lax.all_gather(in_weight, 'seq', axis=0, tiled=True)  81.2 us
    all_gather x1, waiting for transfers between devices, body(): features = lax.all_gather(own_feats, 'tp', axis=1, tiled=True)  27.9 us
    all_to_all x1, starting transfers between devices, body(): lax.all_to_all(jnp.stack([out_weight] * lax.axis_size('seq')), 'seq', 0, 0)  13.2 us
    dot_general x1, matrix products, body(): jnp.einsum('td,dsc->tsc', normed, lax.all_gather(in_weight, 'seq', axis=0...  10.5 us
    ppermute x2, starting transfers between devices, from_behind(): return lax.ppermute(block, axis, route)  7.39 us
    dot_general x1, matrix products, body(): jnp.dot(gated, jnp.concatenate(lax.all_to_all(jnp.stack([out_weight] * la...  7.3 us
  transfers between devices with their start and end apart: 6, of which 4 were waited for; matrix products, arithmetic and copies ran while one was open for 16% of the time, Pallas kernels for 0%

profile of v1, /device:TPU:1, one launch (start us, length us, event | category | flops | bytes accessed | tf_op | source)
XLA Modules:
  0.0 305.5 jit_solution(14422530721791581817)
XLA Ops:
  6.5 1.0 copy-done
  7.6 2.4 fusion.23
  10.1 0.7 all-gather.5.cloned.1.call-update
  10.8 2.4 stack.2
  13.1 13.2 %all-to-all-start = ((bf16[64,512,32]{1,2,0:T(8,128)(2,1)}), bf16[64,512,32]{1,2,0:T(8,128)(2,1)}, u32[]{:S(2)}, u32[]{:S(2)}) async-start(bf16[64,512,32]{1,2,0:T(8,128)(2,1)} %stack.2), calls=%async_computation | async-start | bytes 4194304 | tf_op jit(solution)/shard_map/all_to_all | solution.py:83
  26.3 0.0 all-reduce.2.cloned.1.call-start
  26.5 5.1 %fusion.3 = bf16[128,128,32]{1,2,0:T(8,128)(2,1)} fusion(s32[128,128]{1,0:T(8,128)S(1)} %iota_subtract_fusion, bf16[32,128]{1,0:T(8,128)(2,1)S(1)} %copy-done.7), kind=kOutput, calls=%fused_computation.7 | convolution fusion | flops 136314880 | bytes 1122304 | tf_op jit(solution)/shard_map/isj,gj->gis/dot_general | solution.py:67
  31.6 5.1 %fusion.4 = bf16[128,128,32]{1,2,0:T(8,128)(2,1)} fusion(s32[128,128]{1,0:T(8,128)S(1)} %broadcast_add_fusion, bf16[32,128]{1,0:T(8,128)(2,1)S(1)} %copy-done.7), kind=kOutput, calls=%fused_computation.8 | convolution fusion | flops 136314880 | bytes 1122304 | tf_op jit(solution)/shard_map/isj,gj->gis/dot_general | solution.py:68
  36.7 27.9 %all-gather.3.cloned.1.call-done = bf16[1024,2048]{1,0:T(8,128)(2,1)} async-done(((bf16[1024,512]{1,0:T(8,128)(2,1)}), bf16[1024,2048]{1,0:T(8,128)(2,1)}) %all-gather.3.cloned.1.call-update) | async-done | bytes 4194320 | tf_op jit(solution)/shard_map/all_gather | solution.py:36
  64.6 3.1 %fusion = f32[1024]{0:T(1024)S(1)} fusion(bf16[1024,2048]{1,0:T(8,128)(2,1)} %all-gather.3.cloned.1.call-done), kind=kLoop, calls=%fused_computation.2 | loop fusion | flops 6290432 | bytes 4198400 | tf_op jit(solution)/shard_map/reduce_sum | solution.py:40
  67.7 81.2 %all-gather.5.cloned.1.call-done = bf16[2048,3,512]{2,0,1:T(8,128)(2,1)} async-done(((bf16[32,3,512]{2,0,1:T(8,128)(2,1)}), bf16[2048,3,512]{2,0,1:T(8,128)(2,1)}) %all-gather.5.cloned.1.call-update) | async-done | bytes 6291472 | tf_op jit(solution)/shard_map/all_gather | solution.py:47
  148.8 10.5 %fusion.17 = bf16[1024,3,512]{2,0,1:T(8,128)(2,1)S(1)} fusion(bf16[2048,3,512]{2,0,1:T(8,128)(2,1)} %all-gather.5.cloned.1.call-done, bf16[1024,2048]{1,0:T(8,128)(2,1)} %all-gather.3.cloned.1.call-done, f32[2048]{0:T(1024)S(1)} %copy-done.8, f32[1024]{0:T(1024)S(1)} %add_rsqrt_fusion), kind=kOutput, calls=%fused_computation.31 | convolution fusion | flops 6452412416 | bytes 13643776 | tf_op jit(solution)/shard_map/td,dsc->tsc/dot_general | solution.py:44
  159.4 2.7 collective-permute-start
  162.2 0.9 collective-permute-done
  163.1 5.6 %multiply_add_fusion = f32[1024,3,512]{2,0,1:T(8,128)S(1)} fusion(bf16[1024,3,512]{2,0,1:T(8,128)(2,1)S(1)} %fusion.17, bf16[6,3,512]{2,0,1:T(8,128)(2,1)S(1)} %collective-permute-done, f32[3,512]{1,0:T(4,128)S(1)} %get-tuple-element.12, f32[3,512]{1,0:T(4,128)S(1)} %get-tuple-element.13, f32[3,512]{1,0:T(4,128)S(1)} %get-tuple-element.14, ...), kind=kLoop, calls=%fused_computation.14 | loop fusion | flops 59768832 | bytes 9498624 | tf_op jit(solution)/shard_map/add | solution.py:18
  168.7 2.7 copy-done.1
  171.3 0.4 fusion.20
  171.7 0.5 copy.13
  172.3 4.7 %collective-permute-start.1 = (bf16[128,512]{1,0:T(8,128)(2,1)S(1)}, bf16[128,512]{1,0:T(8,128)(2,1)S(1)}, u32[]{:S(2)}, u32[]{:S(2)}) collective-permute-start(bf16[128,512]{1,0:T(8,128)(2,1)S(1)} %slice_bitcast_fusion), channel_id=1, source_target_pairs={{0,4},{4,8},{8,12},{12,16},{16,20},{20,24},{24,28},{28,32},{32,36}... | collective-permute-start | bytes 393224 | tf_op jit(solution)/shard_map/ppermute | solution.py:10
  176.9 0.3 copy.30
  177.2 2.1 fusion.25
  179.3 0.4 fusion.41
  179.7 1.1 pad_maximum_fusion.1
  180.7 2.3 copy.15
  183.0 1.5 copy.31
  184.5 2.1 add_bitcast_fusion
  186.6 0.9 copy.17
  187.5 1.5 reshape.65
  189.0 3.0 copy.18
  192.0 7.3 %convolution_convert_fusion = bf16[1024,2048]{1,0:T(8,128)(2,1)} fusion(bf16[512,2048]{0,1:T(8,128)(2,1)} %bitcast.13, f32[1024,1,512]{2,0,1:T(8,128)} %copy.18, bf16[1024,1,512]{2,0,1:T(8,128)(2,1)S(1)} %copy-done.4, f32[1024,3,512]{2,0,1:T(8,128)} %copy-done.1, f32[512]{0:T(512)S(1)} %copy-done.9), kind=kOutput, calls=%fused_computation.21 | convolution fusion | flops 2152202240 | bytes 11536384 | tf_op jit(solution)/shard_map/dot_general | solution.py:80
  199.3 97.2 %all-reduce.2.cloned.1.call-done = bf16[1024,2048]{1,0:T(8,128)(2,1)} async-done(((bf16[1024,2048]{1,0:T(8,128)(2,1)}), bf16[1024,2048]{1,0:T(8,128)(2,1)}) %all-reduce.2.cloned.1.call-update) | async-done | bytes 4194320 | tf_op jit(solution)/shard_map/psum | solution.py:87
  296.5 2.5 add_convert_fusion
  (34 shorter events, 0.2 us)
Async XLA Ops:
  6.5 1.0 copy-start
  6.5 58.0 %all-gather.3.cloned.1.call-start = ((), (), s32[]{:S(2)}) async-start(), calls=%async_computation.1 | async-start | bytes 5242880 | tf_op jit(solution)/shard_map/all_gather | solution.py:36
  10.0 16.4 %copy-start.6 = (f32[7,3,512]{2,0,1:T(8,128)S(1)}, f32[7,3,512]{2,0,1:T(8,128)}, u32[]{:S(2)}) copy-start(f32[7,3,512]{2,0,1:T(8,128)} %param.12) | copy-start | bytes 129028
  10.0 16.5 %copy-start.7 = (bf16[32,128]{1,0:T(8,128)(2,1)S(1)}, bf16[32,128]{1,0:T(8,128)(2,1)}, u32[]{:S(2)}) copy-start(bf16[32,128]{1,0:T(8,128)(2,1)} %param.13) | copy-start | bytes 24580
  10.0 138.8 %all-gather.5.cloned.1.call-start = ((), (), s32[]{:S(2)}) async-start(), calls=%async_computation.2 | async-start | bytes 6389760 | tf_op jit(solution)/shard_map/all_gather | solution.py:47
  13.1 178.9 %all-to-all-start = ((bf16[64,512,32]{1,2,0:T(8,128)(2,1)}), bf16[64,512,32]{1,2,0:T(8,128)(2,1)}, u32[]{:S(2)}, u32[]{:S(2)}) async-start(bf16[64,512,32]{1,2,0:T(8,128)(2,1)} %stack.2), calls=%async_computation | async-start | bytes 4194304 | tf_op jit(solution)/shard_map/all_to_all | solution.py:83
  26.3 270.2 %all-reduce.2.cloned.1.call-start = ((), (), s32[]{:S(2)}) async-start(), calls=%async_computation.3 | async-start | bytes 8388608 | tf_op jit(solution)/shard_map/psum | solution.py:87
  31.6 117.2 %copy-start.8 = (f32[2048]{0:T(1024)S(1)}, f32[2048]{0:T(1024)}, u32[]{:S(2)}) copy-start(f32[2048]{0:T(1024)} %param.10) | copy-start | bytes 24580
  159.4 3.7 %collective-permute-start = (bf16[6,3,512]{2,0,1:T(8,128)(2,1)S(1)}, bf16[6,3,512]{2,0,1:T(8,128)(2,1)S(1)}, u32[]{:S(2)}, u32[]{:S(2)}) collective-permute-start(bf16[6,3,512]{2,0,1:T(8,128)(2,1)S(1)} %slice.86), channel_id=1, source_target_pairs={{0,4},{4,8},{8,12},{12,16},{16,20},{20,24},{24,28},{28,32},{32,36}... | collective-permute-start | bytes 55304 | tf_op jit(solution)/shard_map/ppermute | solution.py:10
  168.7 2.7 copy-start.1
  171.7 5.5 %copy-start.3 = (bf16[1024,1,512]{2,0,1:T(8,128)(2,1)}, bf16[1024,1,512]{2,0,1:T(8,128)(2,1)S(1)}, u32[]{:S(2)}) copy-start(bf16[1024,1,512]{2,0,1:T(8,128)(2,1)S(1)} %fusion.20) | copy-start | bytes 3145732
  172.2 7.1 %copy-start.2 = (f32[1024,3,512]{2,0,1:T(8,128)S(1)}, f32[1024,3,512]{2,0,1:T(8,128)}, u32[]{:S(2)}) copy-start(f32[1024,3,512]{2,0,1:T(8,128)} %copy-done.1) | copy-start | bytes 18874372
  172.3 7.4 %collective-permute-start.1 = (bf16[128,512]{1,0:T(8,128)(2,1)S(1)}, bf16[128,512]{1,0:T(8,128)(2,1)S(1)}, u32[]{:S(2)}, u32[]{:S(2)}) collective-permute-start(bf16[128,512]{1,0:T(8,128)(2,1)S(1)} %slice_bitcast_fusion), channel_id=1, source_target_pairs={{0,4},{4,8},{8,12},{12,16},{16,20},{20,24},{24,28},{28,32},{32,36}... | collective-permute-start | bytes 393224 | tf_op jit(solution)/shard_map/ppermute | solution.py:10
  187.5 4.5 %copy-start.9 = (f32[512]{0:T(512)S(1)}, f32[512]{0:T(512)}, u32[]{:S(2)}) copy-start(f32[512]{0:T(512)} %param.14) | copy-start | bytes 6148
  189.0 3.0 copy-start.4
  199.3 97.2 %copy-start.5 = (bf16[1024,512]{1,0:T(8,128)(2,1)S(1)}, bf16[1024,512]{1,0:T(8,128)(2,1)}, u32[]{:S(2)}) copy-start(bf16[1024,512]{1,0:T(8,128)(2,1)} %fusion.23) | copy-start | bytes 3145732
Sparse Core Ops, SparseCore 0:
  10.1 54.3 all-gather.2
  67.4 81.4 all-gather.4
  199.5 97.0 all-reduce.1
